TPU v7x, 32 devices: a whole 2x2x4 slice. The times are simulated.
32 devices in a mesh: depth: 8 (over y, x, core), tile: 4 (over z).
Axes of the slice: x: 2, y: 2, z: 4, core: 2. Of those that a mesh axis runs over, the one named last changes fastest.
Arguments:
- concentration: float32 [64, 128, 256], P('depth', 'tile'), may hold values from -6 to 6
- velocity: float32 [3, 64, 128, 256], P(None, 'depth', 'tile'), may hold values from -6 to 6
- diffusivity: float32 [64, 128, 256], P('depth', 'tile'), may hold values from 0.02 to 0.15
Outputs:
- picture: float32 [4, 128, 256], P(None, 'tile', 'depth')
All inputs are finite; a program needn't handle non-finite values.
Results may differ from a plain program's by a relative error of at most 0.0003.
Values sent between devices are 32-bit elements; how exact they have to be, the bound alone decides.
A program may use at most 64 MiB of HBM per device.

v0:
```python
import math

import jax
import jax.numpy as jnp
from jax import lax
from jax.sharding import PartitionSpec as P

ADVECT = 0.25


def extended(value, sides, width):
    for axis, dim in sides:
        size, length = (lax.axis_size(axis), value.shape[dim])
        up = [(i, (i + 1) % size) for i in range(size - 1)]
        down = [(j, i) for i, j in up]
        last = lax.slice_in_dim(value, length - width, length, axis=dim)
        leading = lax.slice_in_dim(value, 0, width, axis=dim)
        before = lax.ppermute(last, axis, up)
        after = lax.ppermute(leading, axis, down)
        value = jnp.concatenate([before, value, after], axis=dim)
    return value


def update(padded, velocity, diffusion):
    center = padded[1:-1, 1:-1, 1:-1]
    front_cells = padded[2:, 1:-1, 1:-1]
    back_cells = padded[:-2, 1:-1, 1:-1]
    right_cells = padded[1:-1, 2:, 1:-1]
    left_cells = padded[1:-1, :-2, 1:-1]
    upper_cells = padded[1:-1, 1:-1, 2:]
    lower_cells = padded[1:-1, 1:-1, :-2]
    laplace = (
        front_cells
        + back_cells
        + right_cells
        + left_cells
        + upper_cells
        + lower_cells
        - 6.0 * center
    )
    advect = (
        velocity[0] * (front_cells - back_cells)
        + velocity[1] * (right_cells - left_cells)
        + velocity[2] * (upper_cells - lower_cells)
    )
    return center + diffusion * laplace - 0.5 * ADVECT * advect


def emission(mixed_field, bright):
    return (
        jnp.stack([mixed_field, jnp.tanh(mixed_field), mixed_field * mixed_field - 1.0], 0) * bright
    )


def opacity(mixed_field, depth_total):
    return 2.0 / depth_total * (0.5 + jax.nn.sigmoid(2.0 * mixed_field))


def blend(gathered):
    shades = gathered[:3]
    passes = gathered[3]
    through = jnp.cumprod(passes, axis=0)
    ahead_trans = jnp.concatenate([jnp.ones_like(through[:1]), through[:-1]], 0)
    colors = jnp.sum(shades * ahead_trans[None], axis=1)
    coverage = 1.0 - through[-1]
    return jnp.concatenate([colors, coverage[None]], 0)


def body(concentration, velocity, diffusivity):
    layers = concentration.shape[0]
    depth_total = layers * lax.axis_size("depth")
    bright = math.sqrt(depth_total)
    padded = extended(concentration, (("depth", 0), ("tile", 1)), 1)
    padded = jnp.pad(padded, ((0, 0), (0, 0), (1, 1)))
    mixed_field = update(padded, velocity, diffusivity)
    optical = opacity(mixed_field, depth_total)
    before = jnp.cumsum(optical, axis=0) - optical
    weight = jnp.exp(-before) * (1.0 - jnp.exp(-optical))
    colors = jnp.sum(weight[None] * emission(mixed_field, bright), axis=1)
    passed = jnp.exp(-jnp.sum(optical, axis=0))
    stacked = jnp.concatenate([colors, passed[None]], 0)[:, None]
    picture = blend(lax.all_to_all(stacked, "depth", split_axis=3, concat_axis=1, tiled=True))
    return picture


def solution(mesh):
    return jax.shard_map(
        body,
        mesh=mesh,
        in_specs=(
            P("depth", "tile", None),
            P(None, "depth", "tile", None),
            P("depth", "tile", None),
        ),
        out_specs=P(None, "tile", "depth"),
        check_vma=False,
    )
```

profile of v0, /device:TPU:0, one launch (start us, length us, event | category | flops | bytes accessed | tf_op | source)
XLA Modules:
  0.0 30.4 jit_solution(6963863811603782839)
XLA Ops:
  0.0 0.8 %fusion.20 = (f32[1,32,256]{2,1,0:T(8,128)S(1)}, f32[1,32,256]{2,1,0:T(8,128)S(1)}) fusion(f32[8,32,256]{2,1,0:T(8,128)} %param.3), kind=kLoop, calls=%fused_computation.44 | loop fusion | bytes 131072 | tf_op jit(solution)/shard_map/slice | solution.py:17
  0.8 2.4 %collective-permute-start.1 = (f32[1,32,256]{2,1,0:T(8,128)S(1)}, f32[1,32,256]{2,1,0:T(8,128)S(1)}, u32[]{:S(2)}, u32[]{:S(2)}) collective-permute-start(f32[1,32,256]{2,1,0:T(8,128)S(1)} %get-tuple-element.12), channel_id=1, source_target_pairs={{0,4},{4,8},{8,12},{12,16},{16,20},{20,24},{24,28},{1,5},{5,9},{9,... | collective-permute-start | bytes 98312 | tf_op jit(solution)/shard_map/ppermute | solution.py:18
  3.2 1.3 %collective-permute-start = (f32[1,32,256]{2,1,0:T(8,128)S(1)}, f32[1,32,256]{2,1,0:T(8,128)S(1)}, u32[]{:S(2)}, u32[]{:S(2)}) collective-permute-start(f32[1,32,256]{2,1,0:T(8,128)S(1)} %get-tuple-element.11), channel_id=1, source_target_pairs={{4,0},{8,4},{12,8},{16,12},{20,16},{24,20},{28,24},{5,1},{9,5},{13... | collective-permute-start | bytes 98312 | tf_op jit(solution)/shard_map/ppermute | solution.py:19
  4.5 0.0 copy-start.1
  4.5 1.0 %constant_dynamic-update-slice_fusion.1 = f32[10,32,256]{2,1,0:T(8,128)S(1)} fusion(f32[10,32,256]{2,1,0:T(8,128)S(1)} %constant_dynamic-update-slice_fusion.2, f32[8,32,256]{2,1,0:T(8,128)} %param.3), kind=kLoop, calls=%fused_computation.37 | loop fusion | bytes 524288
  5.6 2.8 %collective-permute-done = f32[1,32,256]{2,1,0:T(8,128)S(1)} collective-permute-done((f32[1,32,256]{2,1,0:T(8,128)S(1)}, f32[1,32,256]{2,1,0:T(8,128)S(1)}, u32[]{:S(2)}, u32[]{:S(2)}) %collective-permute-start) | collective-permute-done | bytes 32800 | tf_op jit(solution)/shard_map/ppermute | solution.py:19
  8.4 1.3 %collective-permute-start.2 = (f32[10,1,256]{2,1,0:T(1,128)S(1)}, f32[10,1,256]{2,1,0:T(1,128)S(1)}, u32[]{:S(2)}, u32[]{:S(2)}) collective-permute-start(f32[10,1,256]{2,1,0:T(1,128)S(1)} %get-tuple-element.8), channel_id=1, source_target_pairs={{1,0},{2,1},{3,2},{5,4},{6,5},{7,6},{9,8},{10,9},{11,10},{13,12},{... | collective-permute-start | bytes 30728 | tf_op jit(solution)/shard_map/ppermute | solution.py:19
  9.7 0.0 copy-start
  9.7 4.7 %collective-permute-start.3 = (f32[10,1,256]{2,1,0:T(1,128)S(1)}, f32[10,1,256]{2,1,0:T(1,128)S(1)}, u32[]{:S(2)}, u32[]{:S(2)}) collective-permute-start(f32[10,1,256]{2,1,0:T(1,128)S(1)} %get-tuple-element.7), channel_id=1, source_target_pairs={{0,1},{1,2},{2,3},{4,5},{5,6},{6,7},{8,9},{9,10},{10,11},{12,13},{... | collective-permute-start | bytes 30728 | tf_op jit(solution)/shard_map/ppermute | solution.py:18
  14.4 1.4 %collective-permute-done.3 = f32[10,1,256]{2,1,0:T(1,128)S(1)} collective-permute-done((f32[10,1,256]{2,1,0:T(1,128)S(1)}, f32[10,1,256]{2,1,0:T(1,128)S(1)}, u32[]{:S(2)}, u32[]{:S(2)}) %collective-permute-start.3) | collective-permute-done | bytes 10272 | tf_op jit(solution)/shard_map/ppermute | solution.py:18
  15.8 0.3 %select_maximum_fusion = f32[10,34,258]{2,1,0:T(8,128)S(1)} fusion(f32[10,1,256]{2,1,0:T(1,128)S(1)} %collective-permute-done.2, f32[10,32,256]{2,1,0:T(8,128)S(1)} %constant_dynamic-update-slice_fusion, f32[10,1,256]{2,1,0:T(1,128)S(1)} %collective-permute-done.3), kind=kLoop, calls=%fused_computation.9 | loop fusion | flops 701760 | bytes 699040 | tf_op jit(solution)/shard_map/concatenate | solution.py:20
  16.1 0.3 %tanh_bitcast_fusion = (f32[1,8,32,256]{3,2,1,0:T(8,128)S(1)}, f32[8,32,256]{2,1,0:T(8,128)S(1)}) fusion(f32[3,8,32,256]{3,2,1,0:T(8,128)S(1)} %copy-done.1, f32[8,32,256]{2,1,0:T(8,128)S(1)} %copy-done, f32[8,32,256]{2,1,0:T(8,128)S(1)} %copy-done.2, f32[10,34,258]{2,1,0:T(8,128)S(1)} %select_maximum_fusion, ...), kind=kLoop, calls=%fused_computation.28 | loop fusion | flops 1507328 | bytes 2772992 | tf_op jit(solution)/shard_map/stack | solution.py:51
  16.4 0.1 add_bitcast_fusion
  16.5 0.3 %fusion.3 = f32[8,32,256]{2,1,0:T(8,128)S(1)} fusion(f32[8,32,256]{2,1,0:T(8,128)S(1)} %get-tuple-element.6), kind=kOutput, calls=%fused_computation.4 | output fusion | flops 1245184 | bytes 524288 | tf_op jit(solution)/shard_map/jit(cumsum)/reduce_window_sum | solution.py:77
  16.9 0.1 fusion.4
  17.0 0.2 copy.13
  17.3 0.3 %reshape.17 = f32[8,1,4096]{2,1,0:T(1,128)S(1)} reshape(f32[256,1,4,32]{3,2,1,0:T(4,128)S(1)} %bitcast_bitcast_fusion) | data formatting | bytes 262144
  17.6 10.1 %all_to_all.15 = f32[8,1,4096]{2,1,0:T(1,128)S(1)} all-to-all(f32[8,1,4096]{2,1,0:T(1,128)S(1)} %reshape.17), channel_id=1, replica_groups=mesh['depth'=8,'tile'=4] {'depth'}, dimensions={0} | all-to-all | bytes 262144 | tf_op jit(solution)/shard_map/all_to_all | solution.py:82
  27.7 0.5 %broadcast.34 = f32[]{:T(128)} broadcast(f32[]{:T(128)} %constant.88), dimensions={} | broadcast | bytes 8 | tf_op jit(solution)/shard_map/all_to_all | solution.py:82
  28.2 1.0 %reduce = f32[8,4096]{1,0:T(8,128)S(1)} reduce(f32[8,1,4096]{2,1,0:T(1,128)S(1)} %all_to_all.15, f32[]{:T(128)} %broadcast.34), dimensions={1}, to_apply=%all_to_all.11.reduce_sub_computation | reduce | bytes 262148 | tf_op jit(solution)/shard_map/all_to_all | solution.py:82
  29.2 0.3 reshape.18
  29.4 0.2 copy.15
  29.7 0.1 fusion.7
  29.8 0.6 %pad_maximum_fusion.5 = f32[4,32,32]{2,1,0:T(8,128)} fusion(f32[1,32,32]{2,1,0:T(8,128)S(1)} %slice_subtract_fusion, f32[3,32,32]{2,1,0:T(8,128)S(1)} %fusion.7), kind=kLoop, calls=%fused_computation.32 | loop fusion | flops 4096 | bytes 32768 | tf_op jit(solution)/shard_map/concatenate | solution.py:66
  (16 shorter events, 0.1 us)
Async XLA Ops:
  0.8 3.7 %collective-permute-start.1 = (f32[1,32,256]{2,1,0:T(8,128)S(1)}, f32[1,32,256]{2,1,0:T(8,128)S(1)}, u32[]{:S(2)}, u32[]{:S(2)}) collective-permute-start(f32[1,32,256]{2,1,0:T(8,128)S(1)} %get-tuple-element.12), channel_id=1, source_target_pairs={{0,4},{4,8},{8,12},{12,16},{16,20},{20,24},{24,28},{1,5},{5,9},{9,... | collective-permute-start | bytes 98312 | tf_op jit(solution)/shard_map/ppermute | solution.py:18
  3.2 5.2 %collective-permute-start = (f32[1,32,256]{2,1,0:T(8,128)S(1)}, f32[1,32,256]{2,1,0:T(8,128)S(1)}, u32[]{:S(2)}, u32[]{:S(2)}) collective-permute-start(f32[1,32,256]{2,1,0:T(8,128)S(1)} %get-tuple-element.11), channel_id=1, source_target_pairs={{4,0},{8,4},{12,8},{16,12},{20,16},{24,20},{28,24},{5,1},{9,5},{13... | collective-permute-start | bytes 98312 | tf_op jit(solution)/shard_map/ppermute | solution.py:19
  4.5 11.6 %copy-start.1 = (f32[3,8,32,256]{3,2,1,0:T(8,128)S(1)}, f32[3,8,32,256]{3,2,1,0:T(8,128)}, u32[]{:S(2)}) copy-start(f32[3,8,32,256]{3,2,1,0:T(8,128)} %param.4) | copy-start | bytes 2359300
  8.4 6.0 %collective-permute-start.2 = (f32[10,1,256]{2,1,0:T(1,128)S(1)}, f32[10,1,256]{2,1,0:T(1,128)S(1)}, u32[]{:S(2)}, u32[]{:S(2)}) collective-permute-start(f32[10,1,256]{2,1,0:T(1,128)S(1)} %get-tuple-element.8), channel_id=1, source_target_pairs={{1,0},{2,1},{3,2},{5,4},{6,5},{7,6},{9,8},{10,9},{11,10},{13,12},{... | collective-permute-start | bytes 30728 | tf_op jit(solution)/shard_map/ppermute | solution.py:19
  9.7 6.4 %copy-start = (f32[8,32,256]{2,1,0:T(8,128)S(1)}, f32[8,32,256]{2,1,0:T(8,128)}, u32[]{:S(2)}) copy-start(f32[8,32,256]{2,1,0:T(8,128)} %param.3) | copy-start | bytes 786436
  9.7 6.4 %copy-start.2 = (f32[8,32,256]{2,1,0:T(8,128)S(1)}, f32[8,32,256]{2,1,0:T(8,128)}, u32[]{:S(2)}) copy-start(f32[8,32,256]{2,1,0:T(8,128)} %param.5) | copy-start | bytes 786436
  9.7 6.1 %collective-permute-start.3 = (f32[10,1,256]{2,1,0:T(1,128)S(1)}, f32[10,1,256]{2,1,0:T(1,128)S(1)}, u32[]{:S(2)}, u32[]{:S(2)}) collective-permute-start(f32[10,1,256]{2,1,0:T(1,128)S(1)} %get-tuple-element.7), channel_id=1, source_target_pairs={{0,1},{1,2},{2,3},{4,5},{5,6},{6,7},{8,9},{9,10},{10,11},{12,13},{... | collective-permute-start | bytes 30728 | tf_op jit(solution)/shard_map/ppermute | solution.py:18
where the time goes:
time: 30.7 us; the launch traced here: 30.4 us
  blocking collectives  10.1 us (33%)
  starting transfers between devices  9.65 us (31%)
  waiting for transfers between devices  4.18 us (14%)
  local copies, waits for them, and re-layouts  3.48 us (11%)
  other arithmetic  2.8 us (9%)
    all_to_all x1, blocking collectives, body(): lax.all_to_all(stacked, 'depth', split_axis=3, concat_axis=1, tiled=True)  10.1 us
    ppermute x2, starting transfers between devices, extended(): before = lax.ppermute(last, axis, up)  7.06 us
    ppermute x2, waiting for transfers between devices, extended(): after = lax.ppermute(leading, axis, down)  2.82 us
    ppermute x2, starting transfers between devices, extended(): after = lax.ppermute(leading, axis, down)  2.58 us
    unnamed x11, local copies, waits for them, and re-layouts  1.71 us
    ppermute x2, waiting for transfers between devices, extended(): before = lax.ppermute(last, axis, up)  1.36 us
    all_to_all x1, other arithmetic, body(): lax.all_to_all(stacked, 'depth', split_axis=3, concat_axis=1, tiled=True)  0.95 us
    slice x1, local copies, waits for them, and re-layouts, extended(): leading = lax.slice_in_dim(value, 0, width, axis=dim)  0.78 us
  transfers between devices with their start and end apart: 4, of which 2 were waited for; matrix products, arithmetic and copies ran while one was open for 3% of the time, Pallas kernels for 0%

commit v1 on v0

v1 whole, which is shorter than its diff:
```python
import functools
import math

import jax
import jax.numpy as jnp
from jax import lax
from jax.experimental import pallas as pl
from jax.experimental.pallas import tpu as pltpu
from jax.sharding import PartitionSpec as P

ADVECT = 0.25
LANES = 128
ROWS = 8
SLOT = LANES // 4


def kernel(
    n,
    tiles,
    conc_hbm,
    vel_hbm,
    diff_hbm,
    out_ref,
    conc,
    vel,
    diff,
    field,
    middle,
    z_before,
    z_after,
    x_edge,
    x_before,
    x_after,
    send,
    recv,
    load_sem,
    halo_send,
    halo_recv,
    part_send,
    part_recv,
):
    layers, width, rays = diff.shape
    groups = width // ROWS
    own = rays // n
    total = layers * n
    half = 0.5 * ADVECT
    bright = math.sqrt(total)
    me = lax.axis_index("depth")
    lane_block = lax.axis_index("tile")
    first, last = me == 0, me == n - 1
    left, right = lane_block == 0, lane_block == tiles - 1

    load_conc = pltpu.make_async_copy(
        conc_hbm, conc.at[:, pl.ds(ROWS, width), :], load_sem.at[0]
    )
    load_conc.start()
    barrier = pltpu.get_barrier_semaphore()
    for k in range(1, n):
        pl.semaphore_signal(
            barrier,
            inc=1,
            device_id={"depth": lax.rem(me + k, n)},
            device_id_type=pl.DeviceIdType.MESH,
        )

    @pl.when(jnp.logical_not(left))
    def _():
        pl.semaphore_signal(
            barrier,
            inc=1,
            device_id={"tile": lane_block - 1},
            device_id_type=pl.DeviceIdType.MESH,
        )

    @pl.when(jnp.logical_not(right))
    def _():
        pl.semaphore_signal(
            barrier,
            inc=1,
            device_id={"tile": lane_block + 1},
            device_id_type=pl.DeviceIdType.MESH,
        )

    load_vel = pltpu.make_async_copy(vel_hbm, vel, load_sem.at[1])
    load_vel.start()
    load_diff = pltpu.make_async_copy(diff_hbm, diff, load_sem.at[2])
    load_diff.start()

    zero_rows = jnp.zeros((ROWS, rays), jnp.float32)
    for z in range(layers):
        conc[z, pl.ds(0, ROWS), :] = zero_rows
        conc[z, pl.ds(ROWS + width, ROWS), :] = zero_rows

    @pl.when(first)
    def _():
        z_before[...] = jnp.zeros_like(z_before)

    @pl.when(last)
    def _():
        z_after[...] = jnp.zeros_like(z_after)

    @pl.when(left)
    def _():
        x_before[...] = jnp.zeros_like(x_before)

    @pl.when(right)
    def _():
        x_after[...] = jnp.zeros_like(x_after)

    load_conc.wait()
    for z in range(layers):
        x_edge[0, pl.ds(z, 1), :] = conc[z, pl.ds(ROWS, 1), :]
        x_edge[1, pl.ds(z, 1), :] = conc[z, pl.ds(ROWS + width - 1, 1), :]

    def halo(index, source, target, device):
        return pltpu.make_async_remote_copy(
            src_ref=source,
            dst_ref=target,
            send_sem=halo_send.at[index],
            recv_sem=halo_recv.at[index],
            device_id=device,
            device_id_type=pl.DeviceIdType.MESH,
        )

    inner = pl.ds(ROWS, width)
    deeper = halo(0, conc.at[layers - 1, inner], z_before, {"depth": lax.rem(me + 1, n)})
    nearer = halo(1, conc.at[0, inner], z_after, {"depth": lax.rem(me + n - 1, n)})
    rightward = halo(2, x_edge.at[1], x_before, {"tile": lax.rem(lane_block + 1, tiles)})
    leftward = halo(3, x_edge.at[0], x_after, {"tile": lax.rem(lane_block + tiles - 1, tiles)})

    beside = jnp.where(left, 0, 1) + jnp.where(right, 0, 1)
    pl.semaphore_wait(barrier, n - 1 + beside)

    @pl.when(jnp.logical_not(last))
    def _():
        deeper.start()

    @pl.when(jnp.logical_not(first))
    def _():
        nearer.start()

    @pl.when(jnp.logical_not(right))
    def _():
        rightward.start()

    @pl.when(jnp.logical_not(left))
    def _():
        leftward.start()

    load_vel.wait()
    load_diff.wait()

    lane = lax.broadcasted_iota(jnp.int32, (ROWS, rays), 1)
    row = lax.broadcasted_iota(jnp.int32, (ROWS, rays), 0)

    def local_update(z, start):
        rows = pl.ds(start, ROWS)
        here = conc[z, pl.ds(ROWS + start, ROWS), :]
        left_cells = conc[z, pl.ds(ROWS + start - 1, ROWS), :]
        right_cells = conc[z, pl.ds(ROWS + start + 1, ROWS), :]
        lower_cells = jnp.where(lane == 0, 0.0, pltpu.roll(here, 1, 1))
        upper_cells = jnp.where(lane == rays - 1, 0.0, pltpu.roll(here, rays - 1, 1))
        spread = left_cells + right_cells + lower_cells + upper_cells
        flow = vel[1, z, rows, :] * (right_cells - left_cells) + vel[2, z, rows, :] * (
            upper_cells - lower_cells
        )
        if z > 0:
            back = conc[z - 1, pl.ds(ROWS + start, ROWS), :]
            spread = spread + back
        if z < layers - 1:
            front = conc[z + 1, pl.ds(ROWS + start, ROWS), :]
            spread = spread + front
        if 0 < z < layers - 1:
            slope = front - back
        elif z > 0:
            slope = -back
        else:
            slope = front
        flow = flow + vel[0, z, rows, :] * slope
        return here + diff[z, rows, :] * (spread - 6.0 * here) - half * flow

    def shade(mixed):
        bend = jnp.tanh(mixed)
        passed = jnp.exp((bend + 2.0) * (-1.0 / total))
        return bend, passed

    def add_cell(state, mixed):
        bend, passed = shade(mixed)
        if state is None:
            weight = 1.0 - passed
            return weight * mixed, weight * bend, weight * (mixed * mixed - 1.0), passed
        one, two, three, through = state
        weight = through * (1.0 - passed)
        return (
            one + weight * mixed,
            two + weight * bend,
            three + weight * (mixed * mixed - 1.0),
            through * passed,
        )

    order = list(range(1, groups - 1)) + [0, groups - 1]
    for g in order:
        start = g * ROWS
        edge = g in (0, groups - 1)
        state = None
        for z in range(layers):
            mixed = local_update(z, start)
            if edge or z in (0, layers - 1):
                field[z, pl.ds(start, ROWS), :] = mixed
            else:
                state = add_cell(state, mixed)
        if not edge:
            for c in range(4):
                middle[c, pl.ds(start, ROWS), :] = state[c]

    @pl.when(jnp.logical_not(first))
    def _():
        deeper.wait_recv()

    @pl.when(jnp.logical_not(last))
    def _():
        nearer.wait_recv()

    slot_of = lax.broadcasted_iota(jnp.int32, (ROWS, LANES), 1) // SLOT

    def pack(state, d):
        tile, offset = divmod(d * own, LANES)
        block = None
        for c in range(4):
            piece = state[c][:, tile * LANES : (tile + 1) * LANES]
            shift = (SLOT * c - offset) % LANES
            if shift:
                piece = pltpu.roll(piece, shift, 1)
            block = piece if block is None else jnp.where(slot_of == c, piece, block)
        return block

    def part(g, k):
        target = lax.rem(me + k, n)
        return pltpu.make_async_remote_copy(
            src_ref=send.at[g, target],
            dst_ref=recv.at[g, me],
            send_sem=part_send.at[g, k],
            recv_sem=part_recv.at[g, k],
            device_id={"depth": target},
            device_id_type=pl.DeviceIdType.MESH,
        )

    def corrected(z, start):
        rows = pl.ds(start, ROWS)
        mixed = field[z, rows, :]
        spread = diff[z, rows, :]
        if z == 0:
            mixed = mixed + z_before[rows, :] * (spread + half * vel[0, z, rows, :])
        if z == layers - 1:
            mixed = mixed + z_after[rows, :] * (spread - half * vel[0, z, rows, :])
        if start == 0:
            beside = jnp.where(row == 0, x_before[pl.ds(z, 1), :], 0.0)
            mixed = mixed + beside * (spread + half * vel[1, z, rows, :])
        if start == width - ROWS:
            beside = jnp.where(row == ROWS - 1, x_after[pl.ds(z, 1), :], 0.0)
            mixed = mixed + beside * (spread - half * vel[1, z, rows, :])
        return mixed

    waited = False
    for g in order:
        start = g * ROWS
        edge = g in (0, groups - 1)
        if edge and not waited:
            waited = True

            @pl.when(jnp.logical_not(left))
            def _():
                rightward.wait_recv()

            @pl.when(jnp.logical_not(right))
            def _():
                leftward.wait_recv()

        state = add_cell(None, corrected(0, start))
        if edge:
            for z in range(1, layers):
                state = add_cell(state, corrected(z, start))
        else:
            rows = pl.ds(start, ROWS)
            through = state[3]
            state = tuple(state[c] + through * middle[c, rows, :] for c in range(3)) + (
                through * middle[3, rows, :],
            )
            state = add_cell(state, corrected(layers - 1, start))
        state = tuple(bright * state[c] for c in range(3)) + (state[3],)
        for d in range(n):
            send[g, d] = pack(state, d)
        for k in range(n - 1, 0, -1):
            part(g, k).start()

    for g in order:
        recv[g, me] = send[g, me]

    for g in order:
        for k in range(1, n):
            part(g, k).wait_recv()
        through = None
        for s in range(n):
            block = recv[g, s]
            passed = jnp.where(slot_of >= 2, block, pltpu.roll(block, LANES // 2, 1))
            passed = jnp.where(slot_of % 2 == 1, passed, pltpu.roll(passed, LANES - SLOT, 1))
            if through is None:
                picture, through = block, passed
            else:
                picture, through = picture + through * block, through * passed
        rows = pl.ds(g * ROWS, ROWS)
        for c in range(3):
            color = pltpu.roll(picture, LANES - SLOT * c, 1) if c else picture
            out_ref[c, rows, :] = color[:, :own]
        out_ref[3, rows, :] = (1.0 - through)[:, :own]

    @pl.when(jnp.logical_not(last))
    def _():
        deeper.wait_send()

    @pl.when(jnp.logical_not(first))
    def _():
        nearer.wait_send()

    @pl.when(jnp.logical_not(right))
    def _():
        rightward.wait_send()

    @pl.when(jnp.logical_not(left))
    def _():
        leftward.wait_send()

    for g in order:
        for k in range(1, n):
            part(g, k).wait_send()


def solution(mesh):
    n, tiles = mesh.shape["depth"], mesh.shape["tile"]

    def body(concentration, velocity, diffusivity):
        layers, width, rays = concentration.shape
        groups = width // ROWS
        own = rays // n
        assert own <= SLOT and LANES % own == 0
        scratch = [
            pltpu.VMEM((layers, width + 2 * ROWS, rays), jnp.float32),
            pltpu.VMEM(velocity.shape, jnp.float32),
            pltpu.VMEM(diffusivity.shape, jnp.float32),
            pltpu.VMEM((layers, width, rays), jnp.float32),
            pltpu.VMEM((4, width, rays), jnp.float32),
            pltpu.VMEM((width, rays), jnp.float32),
            pltpu.VMEM((width, rays), jnp.float32),
            pltpu.VMEM((2, layers, rays), jnp.float32),
            pltpu.VMEM((layers, rays), jnp.float32),
            pltpu.VMEM((layers, rays), jnp.float32),
            pltpu.VMEM((groups, n, ROWS, LANES), jnp.float32),
            pltpu.VMEM((groups, n, ROWS, LANES), jnp.float32),
            pltpu.SemaphoreType.DMA((3,)),
            pltpu.SemaphoreType.DMA((4,)),
            pltpu.SemaphoreType.DMA((4,)),
            pltpu.SemaphoreType.DMA((groups, n)),
            pltpu.SemaphoreType.DMA((groups, n)),
        ]
        return pl.pallas_call(
            functools.partial(kernel, n, tiles),
            out_shape=jax.ShapeDtypeStruct((4, width, own), jnp.float32),
            in_specs=[pl.BlockSpec(memory_space=pl.ANY)] * 3,
            out_specs=pl.BlockSpec(memory_space=pltpu.VMEM),
            scratch_shapes=scratch,
            compiler_params=pltpu.CompilerParams(collective_id=0, has_side_effects=True),
        )(concentration, velocity, diffusivity)

    return jax.shard_map(
        body,
        mesh=mesh,
        in_specs=(
            P("depth", "tile", None),
            P(None, "depth", "tile", None),
            P("depth", "tile", None),
        ),
        out_specs=P(None, "tile", "depth"),
        check_vma=False,
    )
```

time: 30.7 us -> 14 us (0.46)
  Pallas kernels: 0 us -> 12.3 us
  blocking collectives: 10.1 us -> 0 us
  starting transfers between devices: 9.65 us -> 0 us
  waiting for transfers between devices: 4.18 us -> 0 us
  other arithmetic: 2.8 us -> 0 us
  local copies, waits for them, and re-layouts: 3.48 us -> 1.47 us
    pallas_call x0 -> x1, Pallas kernels: none -> 12.3 us  [body(): pl.pallas_call(functools.partial(kernel, n, tiles), out_shape=jax.ShapeDt...]
    all_to_all x1 -> x0, blocking collectives: 10.1 us -> none  [body(): lax.all_to_all(stacked, 'depth', split_axis=3, concat_axis=1, tiled=True)]
    ppermute x4 -> x0, starting transfers between devices: 9.65 us -> none  [the longest x2 7.06 us: extended(): before = lax.ppermute(last, axis, up)]
    ppermute x4 -> x0, waiting for transfers between devices: 4.18 us -> none  [the longest x2 2.82 us: extended(): after = lax.ppermute(leading, axis, down)]
    concatenate x3 -> x0, other arithmetic: 0.95 us -> none  [the longest x1 0.64 us: blend(): return jnp.concatenate([colors, coverage[None]], 0)]
    all_to_all x1 -> x0, other arithmetic: 0.95 us -> none  [body(): lax.all_to_all(stacked, 'depth', split_axis=3, concat_axis=1, tiled=True)]
    slice x3 -> x0, local copies, waits for them, and re-layouts: 0.8 us -> none  [the longest x1 0.78 us: extended(): leading = lax.slice_in_dim(value, 0, width, axis=dim)]
    another operation x4 -> x0, other arithmetic: 0.74 us -> none  [the longest x2 0.41 us: emission(): jnp.stack([mixed_field, jnp.tanh(mixed_field), mixed_field * mixed_field...]
  transfers between devices with their start and end apart: 4 -> 0, of which waited for: 2 -> 0; matrix products, arithmetic and copies ran while one was open for 3% -> 0% of each run, Pallas kernels for 0% -> 0%
where the time goes in v1:
time: 14 us; the launch traced here: 13.8 us
  Pallas kernels  12.3 us (88%)
  local copies, waits for them, and re-layouts  1.47 us (10%)
    pallas_call x1, Pallas kernels, body(): pl.pallas_call(functools.partial(kernel, n, tiles), out_shape=jax.ShapeDt...  12.3 us
    unnamed x1, local copies, waits for them, and re-layouts  1.47 us

profile of v1, /device:TPU:0, one launch (start us, length us, event | category | flops | bytes accessed | tf_op | source)
XLA Modules:
  0.0 13.8 jit_solution(6108343763102789417)
XLA Ops:
  0.0 12.3 %shard_map.37 = f32[4,32,32]{2,1,0:T(8,128)} custom-call(f32[8,32,256]{2,1,0:T(8,128)} %conc_hbm.1, f32[3,8,32,256]{3,2,1,0:T(8,128)} %vel_hbm.1, f32[8,32,256]{2,1,0:T(8,128)} %diff_hbm.1), custom_call_target="tpu_custom_call" | custom-call | tf_op jit(solution)/shard_map/pallas_call | solution.py:365
  12.3 1.5 %copy.5 = f32[4,32,32]{2,1,0:T(8,128)} copy(f32[4,32,32]{2,1,0:T(8,128)} %shard_map.37) | data formatting | bytes 32768

commit v2 on v1

--- a/solution.py
+++ b/solution.py
@@ -368,8 +368,8 @@
             in_specs=[pl.BlockSpec(memory_space=pl.ANY)] * 3,
             out_specs=pl.BlockSpec(memory_space=pltpu.VMEM),
             scratch_shapes=scratch,
-            compiler_params=pltpu.CompilerParams(collective_id=0, has_side_effects=True),
-        )(concentration, velocity, diffusivity)
+            compiler_params=pltpu.CompilerParams(collective_id=0, has_side_effects=True, vmem_limit_bytes=16 << 20),
+        )(*[pltpu.with_memory_space_constraint(v, pltpu.HBM) for v in (concentration, velocity, diffusivity)])
 
     return jax.shard_map(
         body,

time: 14 us -> 12.5 us (0.89)
  local copies, waits for them, and re-layouts: 1.47 us -> 0.63 us
  Pallas kernels: 12.3 us -> 11.7 us
    unnamed x1, local copies, waits for them, and re-layouts: 1.47 us -> 0.63 us
    pallas_call x1, Pallas kernels: 12.3 us -> 11.7 us  [body(): pl.pallas_call(functools.partial(kernel, n, tiles), out_shape=jax.ShapeDt...]
where the time goes in v2:
time: 12.5 us; the launch traced here: 12.4 us
  Pallas kernels  11.7 us (94%)
  local copies, waits for them, and re-layouts  0.63 us (5%)
    pallas_call x1, Pallas kernels, body(): pl.pallas_call(functools.partial(kernel, n, tiles), out_shape=jax.ShapeDt...  11.7 us
    unnamed x1, local copies, waits for them, and re-layouts  0.63 us

profile of v2, /device:TPU:0, one launch (start us, length us, event | category | flops | bytes accessed | tf_op | source)
XLA Modules:
  0.0 12.4 jit_solution(1498680167403275591)
XLA Ops:
  0.0 11.7 %shard_map.37 = f32[4,32,32]{2,1,0:T(8,128)S(1)} custom-call(f32[8,32,256]{2,1,0:T(8,128)} %conc_hbm.1, f32[3,8,32,256]{3,2,1,0:T(8,128)} %vel_hbm.1, f32[8,32,256]{2,1,0:T(8,128)} %diff_hbm.1), custom_call_target="tpu_custom_call" | custom-call | tf_op jit(solution)/shard_map/pallas_call | solution.py:365
  11.7 0.6 %copy.5 = f32[4,32,32]{2,1,0:T(8,128)} copy(f32[4,32,32]{2,1,0:T(8,128)S(1)} %shard_map.37) | data formatting | bytes 32768

commit v3 on v2

--- a/solution.py
+++ b/solution.py
@@ -131,6 +131,14 @@
     beside = jnp.where(left, 0, 1) + jnp.where(right, 0, 1)
     pl.semaphore_wait(barrier, n - 1 + beside)
 
+    @pl.when(jnp.logical_not(right))
+    def _():
+        rightward.start()
+
+    @pl.when(jnp.logical_not(left))
+    def _():
+        leftward.start()
+
     @pl.when(jnp.logical_not(last))
     def _():
         deeper.start()
@@ -138,14 +146,6 @@
     @pl.when(jnp.logical_not(first))
     def _():
         nearer.start()
-
-    @pl.when(jnp.logical_not(right))
-    def _():
-        rightward.start()
-
-    @pl.when(jnp.logical_not(left))
-    def _():
-        leftward.start()
 
     load_vel.wait()
     load_diff.wait()
@@ -290,7 +290,7 @@
         state = tuple(bright * state[c] for c in range(3)) + (state[3],)
         for d in range(n):
             send[g, d] = pack(state, d)
-        for k in range(n - 1, 0, -1):
+        for k in range(1, n):
             part(g, k).start()
 
     for g in order:

time: 12.5 us -> 12.4 us (level)
    pallas_call x1, Pallas kernels: 11.7 us -> 11.6 us  [body(): pl.pallas_call(functools.partial(kernel, n, tiles), out_shape=jax.ShapeDt...]
where the time goes in v3:
time: 12.4 us; the launch traced here: 12.2 us
  Pallas kernels  11.6 us (94%)
  local copies, waits for them, and re-layouts  0.63 us (5%)
    pallas_call x1, Pallas kernels, body(): pl.pallas_call(functools.partial(kernel, n, tiles), out_shape=jax.ShapeDt...  11.6 us
    unnamed x1, local copies, waits for them, and re-layouts  0.63 us

profile of v3, /device:TPU:0, one launch (start us, length us, event | category | flops | bytes accessed | tf_op | source)
XLA Modules:
  0.0 12.2 jit_solution(14720783181551774016)
XLA Ops:
  0.0 11.6 %shard_map.37 = f32[4,32,32]{2,1,0:T(8,128)S(1)} custom-call(f32[8,32,256]{2,1,0:T(8,128)} %conc_hbm.1, f32[3,8,32,256]{3,2,1,0:T(8,128)} %vel_hbm.1, f32[8,32,256]{2,1,0:T(8,128)} %diff_hbm.1), custom_call_target="tpu_custom_call" | custom-call | tf_op jit(solution)/shard_map/pallas_call | solution.py:365
  11.6 0.6 %copy.5 = f32[4,32,32]{2,1,0:T(8,128)} copy(f32[4,32,32]{2,1,0:T(8,128)S(1)} %shard_map.37) | data formatting | bytes 32768
